TPU v7x, 32 devices: a whole 2x2x4 slice. The times are simulated.
32 devices in a mesh: order: 4 (over y, x), chan: 8 (over z, core).
Axes of the slice: x: 2, y: 2, z: 4, core: 2. Of those that a mesh axis runs over, the one named last changes fastest.
Arguments:
- grad_out: bfloat16 [3, 256, 720, 1440], P(None, 'chan', 'order'), may hold values from -6 to 6
- legendre: bfloat16 [48, 720, 768], P('order', 'chan'), as said below
- filter_re: float32 [256, 720], P('chan'), may hold values from -6 to 6
- filter_im: float32 [256, 720], P('chan'), may hold values from -6 to 6
- quad_weight: float32 [720], P('order'), may hold values from 0.5 to 2
- pair_order: int32 [48], replicated, may hold values from 0 to 359, as said below
Outputs:
- grad_in: bfloat16 [3, 256, 720, 1440], P(None, 'chan', 'order')
Inputs may be any that keep to these rules, and one draw needn't show every extreme that they name: `pair_order`: the values are distinct. Slot j belongs to index j // 12 of order. `legendre`: entries in rows r > 720 of the last dimension are zero.
All inputs are finite; a program needn't handle non-finite values.
Results may differ from a plain program's by a relative error of at most 0.0072.
Values may be sent and summed in bfloat16 or wider, within the bound.
A program may use at most 256 MiB of HBM per device.

v0:
```python
import math

import jax
import jax.numpy as jnp
from jax import lax
from jax.sharding import PartitionSpec as P

NLON = 1440
M = 720


def basis_tables(pair_order):
    high_order = M - 1 - pair_order
    orders = jnp.stack([pair_order, pair_order, high_order, high_order], axis=1).reshape(-1)
    columns = orders.shape[0]
    parity = jnp.arange(columns, dtype=jnp.int32) % 2
    longitude = jnp.arange(NLON, dtype=jnp.int32)
    phases = longitude[:, None] * orders[None, :] % NLON
    angles = phases.astype(jnp.float32) * (2.0 * math.pi / NLON)
    fourier = jnp.where(parity[None, :] == 0, jnp.cos(angles), -jnp.sin(angles))
    factor = jnp.where(orders == 0, 1.0, 2.0).astype(jnp.float32)
    forward = (fourier * factor[None, :]).astype(jnp.bfloat16)
    inverse = fourier.T.astype(jnp.bfloat16)
    return (forward, inverse)


def pair_gains(low_order, filter_re, filter_im, packed_rows):
    both = jnp.stack([filter_re, filter_im], axis=0)
    channels = both.shape[1]
    padded = jnp.concatenate([both, jnp.zeros((2, channels, packed_rows), jnp.float32)], axis=2)
    tail = jnp.broadcast_to(both[:, :, M - 1 : M], (2, channels, packed_rows - 1 - M))
    shifted = jnp.concatenate([both[:, :, :1], both, tail], axis=2)
    row_ids = jnp.arange(packed_rows, dtype=jnp.int32)
    below = row_ids[None, :] < (M - low_order)[:, None]
    gathered_rows = []
    for index in range(low_order.shape[0]):
        upper = lax.dynamic_slice_in_dim(padded, low_order[index], packed_rows, 2)
        gathered_rows.append(jnp.where(below[index][None, None, :], upper, shifted))
    gains = jnp.stack(gathered_rows, axis=1)
    return (below, jnp.transpose(gains, (0, 1, 3, 2)))


def filter_split(spectrum, low_order, filter_re, filter_im):
    pairs_dev, packed_rows = (spectrum.shape[0], spectrum.shape[1])
    below, gains = pair_gains(low_order, filter_re, filter_im, packed_rows)
    gain_re = gains[0][:, :, None, :]
    gain_im = gains[1][:, :, None, :]
    inside = below[:, :, None, None]
    former = jnp.where(inside, spectrum[:, :, 0], spectrum[:, :, 2])
    latter = jnp.where(inside, spectrum[:, :, 1], spectrum[:, :, 3])
    real_part = gain_re * former + gain_im * latter
    imag_part = gain_re * latter - gain_im * former
    keep_mask = inside.astype(real_part.dtype)
    split = jnp.stack(
        [
            real_part * keep_mask,
            imag_part * keep_mask,
            real_part * (1.0 - keep_mask),
            imag_part * (1.0 - keep_mask),
        ],
        axis=2,
    )
    return split.astype(jnp.bfloat16).reshape(pairs_dev, packed_rows, -1)


def body(grad_out, legendre, filter_re, filter_im, quad_weight, pair_order):
    samples, channels, lat_local, longitudes = grad_out.shape
    pairs_dev = legendre.shape[0]
    packed_rows = legendre.shape[2]
    pairs_all = pair_order.shape[0]
    forward, inverse = basis_tables(pair_order)
    forward = forward.reshape(longitudes, pairs_all, 4)
    coeffs = jnp.einsum("sctl,lpq->ptqsc", grad_out, forward, preferred_element_type=jnp.float32)
    coeffs = coeffs.astype(jnp.bfloat16).reshape(pairs_all, lat_local, 4 * samples * channels)
    gathered = lax.all_to_all(coeffs, "order", split_axis=0, concat_axis=1, tiled=True)
    start_slot = lax.axis_index("order") * pairs_dev
    low_order = lax.dynamic_slice_in_dim(pair_order, start_slot, pairs_dev)
    whole = None
    whole = lax.all_gather(legendre, "chan", axis=1, tiled=True)
    spectrum = jnp.einsum("ptr,ptx->prx", whole, gathered, preferred_element_type=jnp.float32)
    spectrum = spectrum.reshape(pairs_dev, packed_rows, 4, samples, channels)
    split = filter_split(spectrum, low_order, filter_re, filter_im)
    synthesis = jnp.einsum("ptr,prx->ptx", whole, split, preferred_element_type=jnp.float32)
    synthesis = synthesis.astype(jnp.bfloat16)
    local_band = lax.all_to_all(synthesis, "order", split_axis=1, concat_axis=0, tiled=True)
    local_band = local_band.reshape(pairs_all, lat_local, 4, samples, channels)
    inverse = inverse.reshape(pairs_all, 4, longitudes)
    values = jnp.einsum("ptqsc,pql->sctl", local_band, inverse, preferred_element_type=jnp.float32)
    scale = quad_weight * (2.0 * math.pi / NLON)
    return (values * scale[None, None, :, None]).astype(jnp.bfloat16)


def solution(mesh):
    in_specs = (
        P(None, "chan", "order", None),
        P("order", "chan", None),
        P("chan", None),
        P("chan", None),
        P("order"),
        P(),
    )
    out_specs = P(None, "chan", "order", None)
    return jax.shard_map(body, mesh=mesh, in_specs=in_specs, out_specs=out_specs, check_vma=False)
```

profile of v0, /device:TPU:0, one launch (start us, length us, event | category | flops | bytes accessed | tf_op | source)
XLA Modules:
  0.0 447.9 jit_solution(17455911214528204717)
XLA Ops:
  6.5 3.8 copy.21
  10.4 5.6 %fusion.103 = bf16[1440,48,4,1,1]{0,1,4,3,2:T(8,128)(2,1)S(1)} fusion(f32[48,4]{0,1:T(4,128)S(1)} %compare_select_fusion, s32[48,4]{0,1:T(4,128)S(1)} %pad_add_fusion, pred[48,4]{0,1:T(4,128)(4,1)S(1)} %fusion.85), kind=kLoop, calls=%fused_computation.54.clone.clone.1 | loop fusion | flops 3594240 | bytes 554688 | tf_op jit(solution)/shard_map/sctl,lpq->ptqsc/dot_general | solution.py:73
  16.0 53.8 %fusion.13 = bf16[48,4,3,32,180]{4,0,3,2,1:T(8,128)(2,1)} fusion(bf16[3,32,180,1440]{3,1,2,0:T(8,128)(2,1)} %param.6, bf16[1440,48,4,1,1]{0,1,4,3,2:T(8,128)(2,1)S(1)} %fusion.103), kind=kOutput, calls=%fused_computation.13 | convolution fusion | flops 9558466560 | bytes 56954880 | tf_op jit(solution)/shard_map/sctl,lpq->ptqsc/dot_general | solution.py:73
  69.8 12.5 %copy.19 = bf16[48,180,384]{2,1,0:T(8,128)(2,1)} copy(bf16[48,180,384]{1,0,2:T(8,128)(2,1)} %bitcast.154) | data formatting | bytes 13271040 | tf_op jit(solution)/shard_map/reshape | solution.py:74
  82.4 6.0 %all-to-all-start = ((bf16[48,180,384]{2,1,0:T(8,128)(2,1)}), bf16[48,180,384]{2,1,0:T(8,128)(2,1)}, u32[]{:S(2)}, u32[]{:S(2)}) async-start(bf16[48,180,384]{2,1,0:T(8,128)(2,1)} %copy.19), calls=%async_computation | async-start | bytes 13565952 | tf_op jit(solution)/shard_map/all_to_all | solution.py:75
  88.5 0.7 fusion.94
  112.8 0.2 fusion.49
  113.4 0.2 fusion.58
  113.5 0.2 fusion.61
  114.5 0.2 fusion.76
  115.1 49.9 %all-to-all-done = bf16[48,180,384]{2,1,0:T(8,128)(2,1)} async-done(((bf16[48,180,384]{2,1,0:T(8,128)(2,1)}), bf16[48,180,384]{2,1,0:T(8,128)(2,1)}, u32[]{:S(2)}, u32[]{:S(2)}) %all-to-all-start) | async-done | bytes 6635552 | tf_op jit(solution)/shard_map/all_to_all | solution.py:75
  165.0 6.5 %copy.20 = bf16[12,4,180,384]{3,2,1,0:T(8,128)(2,1)} copy(bf16[12,4,180,384]{3,2,0,1:T(8,128)(2,1)} %bitcast.39) | data formatting | bytes 13271040 | tf_op jit(solution)/shard_map/all_to_all | solution.py:75
  171.5 9.8 %all_to_all.27 = bf16[12,720,384]{2,1,0:T(8,128)(2,1)} reshape(bf16[12,4,180,384]{3,2,1,0:T(8,128)(2,1)} %copy.20) | data formatting | bytes 13271040 | tf_op jit(solution)/shard_map/all_to_all | solution.py:75
  181.2 21.0 %fusion.7 = f32[12,384,768]{2,1,0:T(8,128)} fusion(bf16[12,720,384]{2,1,0:T(8,128)(2,1)} %all_to_all.27, bf16[12,720,768]{2,0,1:T(8,128)(2,1)} %all-gather.2.cloned.1.call-done), kind=kOutput, calls=%fused_computation.8 | convolution fusion | flops 5096079360 | bytes 34062336 | tf_op jit(solution)/shard_map/ptr,ptx->prx/dot_general | solution.py:80
  202.2 6.3 %multiply_convert_fusion.3 = (bf16[12,768,1,3,32]{1,4,3,2,0:T(8,128)(2,1)S(1)}, f32[12,768,1,3,32]{1,4,3,2,0:T(8,128)S(1)}, bf16[12,768,1,3,32]{1,4,3,2,0:T(8,128)(2,1)S(1)}, f32[12,768,1,3,32]{1,4,3,2,0:T(8,128)S(1)}) fusion(f32[12,768]{1,0:T(8,128)S(1)} %get-tuple-element.44, f32[12,768,4,3,32]{1,4,3,2,0:T(8,128)} %bitcast.152, ...), kind=kLoop, calls=%fused_computation.21 | loop fusion | flops 10616832 | bytes 27177984 | tf_op jit(solution)/shard_map/convert
  208.5 1.0 multiply_convert_fusion.1
  209.5 3.5 pad_maximum_fusion
  213.0 19.3 %fusion.16 = bf16[12,720,384]{2,1,0:T(8,128)(2,1)} fusion(bf16[12,768,384]{1,2,0:T(8,128)(2,1)} %bitcast.155, bf16[12,720,768]{2,0,1:T(8,128)(2,1)} %all-gather.2.cloned.1.call-done), kind=kOutput, calls=%fused_computation.14 | convolution fusion | flops 5099397120 | bytes 26984448 | tf_op jit(solution)/shard_map/ptr,prx->ptx/dot_general | solution.py:83
  232.3 8.1 %copy.25 = bf16[12,720,384]{2,0,1:T(8,128)(2,1)} copy(bf16[12,720,384]{2,1,0:T(8,128)(2,1)} %fusion.16) | data formatting | bytes 13271040 | tf_op jit(solution)/shard_map/convert_element_type | solution.py:84
  240.4 6.1 %all-to-all-start.1 = ((bf16[12,720,384]{2,0,1:T(8,128)(2,1)}), bf16[12,720,384]{2,0,1:T(8,128)(2,1)}, u32[]{:S(2)}, u32[]{:S(2)}) async-start(bf16[12,720,384]{2,0,1:T(8,128)(2,1)} %copy.25), calls=%async_computation.1 | async-start | bytes 17694720 | tf_op jit(solution)/shard_map/all_to_all | solution.py:85
  246.5 96.8 %all-to-all-done.1 = bf16[12,720,384]{2,0,1:T(8,128)(2,1)} async-done(((bf16[12,720,384]{2,0,1:T(8,128)(2,1)}), bf16[12,720,384]{2,0,1:T(8,128)(2,1)}, u32[]{:S(2)}, u32[]{:S(2)}) %all-to-all-start.1) | async-done | bytes 6635552 | tf_op jit(solution)/shard_map/all_to_all | solution.py:85
  343.4 12.7 %copy.27 = bf16[4,12,180,384]{2,3,1,0:T(8,128)(2,1)} copy(bf16[4,12,180,384]{3,1,2,0:T(8,128)(2,1)} %bitcast.48) | data formatting | bytes 13271040 | tf_op jit(solution)/shard_map/all_to_all | solution.py:85
  356.0 49.0 %fusion.1 = bf16[3,32,180,1440]{3,2,1,0:T(8,128)(2,1)} fusion(f32[180]{0:T(256)S(1)} %broadcast_multiply_fusion, bf16[48,180,4,3,32]{1,4,3,2,0:T(8,128)(2,1)} %bitcast.153, s32[48,4]{0,1:T(4,128)S(1)} %pad_add_fusion, pred[48,4]{0,1:T(4,128)(4,1)S(1)} %fusion.85), kind=kOutput, calls=%fused_computation.2 | convolution fusion | flops 9608232960 | bytes 56403600 | tf_op jit(solution)/shard_map/ptqsc,pql->sctl/dot_general | solution.py:88
  405.0 35.6 %copy.29 = bf16[3,32,180,1440]{3,1,2,0:T(8,128)(2,1)} copy(bf16[3,32,180,1440]{3,2,1,0:T(8,128)(2,1)} %fusion.1) | data formatting | bytes 99532800 | tf_op jit(solution)/shard_map/convert_element_type | solution.py:90
  (32 shorter events, 2.3 us)
Async XLA Ops:
  6.5 3.8 copy-start.2
  6.5 174.7 %all-gather.2.cloned.1.call-start = ((), (), s32[]{:S(2)}) async-start(), calls=%async_computation.2 | async-start | bytes 19906560 | tf_op jit(solution)/shard_map/all_gather | solution.py:79
  82.4 29.7 %copy-start = (f32[32,720]{1,0:T(8,128)S(1)}, f32[32,720]{1,0:T(8,128)}, u32[]{:S(2)}) copy-start(f32[32,720]{1,0:T(8,128)} %param.9) | copy-start | bytes 276484
  82.4 29.7 %copy-start.1 = (f32[32,720]{1,0:T(8,128)S(1)}, f32[32,720]{1,0:T(8,128)}, u32[]{:S(2)}) copy-start(f32[32,720]{1,0:T(8,128)} %param.8) | copy-start | bytes 276484
  82.4 82.6 %all-to-all-start = ((bf16[48,180,384]{2,1,0:T(8,128)(2,1)}), bf16[48,180,384]{2,1,0:T(8,128)(2,1)}, u32[]{:S(2)}, u32[]{:S(2)}) async-start(bf16[48,180,384]{2,1,0:T(8,128)(2,1)} %copy.19), calls=%async_computation | async-start | bytes 13565952 | tf_op jit(solution)/shard_map/all_to_all | solution.py:75
  240.4 6.1 %copy-start.3 = (f32[180]{0:T(256)S(1)}, f32[180]{0:T(256)}, u32[]{:S(2)}) copy-start(f32[180]{0:T(256)} %param.10) | copy-start | bytes 2164
  240.4 103.0 %all-to-all-start.1 = ((bf16[12,720,384]{2,0,1:T(8,128)(2,1)}), bf16[12,720,384]{2,0,1:T(8,128)(2,1)}, u32[]{:S(2)}, u32[]{:S(2)}) async-start(bf16[12,720,384]{2,0,1:T(8,128)(2,1)} %copy.25), calls=%async_computation.1 | async-start | bytes 17694720 | tf_op jit(solution)/shard_map/all_to_all | solution.py:85
Sparse Core Ops, SparseCore 0:
  10.5 161.3 all-gather.1
where the time goes:
time: 457 us; the launch traced here: 448 us
  waiting for transfers between devices  147 us (32%)
  matrix products  143 us (31%)
  local copies, waits for them, and re-layouts  90 us (20%)
  between operations  36.9 us (8%)
  other arithmetic  19 us (4%)
  starting transfers between devices  12.2 us (3%)
    all_to_all x1, waiting for transfers between devices, body(): lax.all_to_all(synthesis, 'order', split_axis=1, concat_axis=0, tiled=True)  96.8 us
    dot_general x1, matrix products, body(): jnp.einsum('sctl,lpq->ptqsc', grad_out, forward, preferred_element_type=j...  53.8 us
    all_to_all x1, waiting for transfers between devices, body(): lax.all_to_all(coeffs, 'order', split_axis=0, concat_axis=1, tiled=True)  49.9 us
    dot_general x1, matrix products, body(): jnp.einsum('ptqsc,pql->sctl', local_band, inverse, preferred_element_type...  49 us
    convert_element_type x1, local copies, waits for them, and re-layouts, body(): return (values * scale[None, None, :, None]).astype(jnp.bfloat16)  35.6 us
    dot_general x1, matrix products, body(): jnp.einsum('ptr,ptx->prx', whole, gathered, preferred_element_type=jnp.fl...  21 us
    dot_general x1, matrix products, body(): jnp.einsum('ptr,prx->ptx', whole, split, preferred_element_type=jnp.float32)  19.3 us
    all_to_all x2, local copies, waits for them, and re-layouts, body(): lax.all_to_all(coeffs, 'order', split_axis=0, concat_axis=1, tiled=True)  16.2 us
  transfers between devices with their start and end apart: 3, of which 2 were waited for; matrix products, arithmetic and copies ran while one was open for 18% of the time, Pallas kernels for 0%

commit v1 on v0

v1 whole, which is shorter than its diff:
```python
import functools
import math

import jax
import jax.numpy as jnp
from jax import lax
from jax.experimental import pallas as pl
from jax.experimental.pallas import tpu as pltpu
from jax.sharding import PartitionSpec as P

NLON = 1440
M = 720


def step_of(count, most):
    return max(d for d in range(1, most + 1) if count % d == 0)


def basis_tables(pair_order, devices, rows):
    low = pair_order.reshape(devices, -1)
    per = low.shape[1]
    orders = jnp.stack([low, low, M - 1 - low, M - 1 - low], axis=1)
    orders = jnp.pad(orders, ((0, 0), (0, 0), (0, rows - per))).reshape(-1)
    shape = (devices, 4, rows)
    real = (lax.broadcasted_iota(jnp.int32, shape, 1) % 2 == 0).reshape(-1)
    live = (lax.broadcasted_iota(jnp.int32, shape, 2) < per).reshape(-1)
    longitude = jnp.arange(NLON, dtype=jnp.int32)

    def table(phases, real, live):
        angles = (phases % NLON).astype(jnp.float32) * (2.0 * math.pi / NLON)
        values = jnp.where(real, jnp.cos(angles), -jnp.sin(angles))
        return jnp.where(live, values, 0.0)

    inverse = table(orders[:, None] * longitude[None, :], real[:, None], live[:, None])
    factor = jnp.where(orders == 0, 1.0, 2.0).astype(jnp.float32)
    forward = (inverse * factor[:, None]).astype(jnp.bfloat16).T
    return forward, inverse.astype(jnp.bfloat16)


def pair_gains(low_order, filter_re, filter_im, packed_rows):
    both = jnp.concatenate([filter_re, filter_im], axis=0).T
    width = both.shape[1]
    padded = jnp.concatenate([both, jnp.zeros((packed_rows, width), jnp.float32)], axis=0)
    tail = jnp.broadcast_to(both[M - 1 : M], (packed_rows - 1 - M, width))
    shifted = jnp.concatenate([both[:1], both, tail], axis=0)
    row_ids = jnp.arange(packed_rows, dtype=jnp.int32)
    below = row_ids[None, :] < (M - low_order)[:, None]
    gathered = []
    for index in range(low_order.shape[0]):
        upper = lax.dynamic_slice_in_dim(padded, low_order[index], packed_rows, 0)
        gathered.append(jnp.where(below[index][:, None], upper, shifted))
    return jnp.stack(gathered, axis=0)


def forward_kernel(x_ref, table_ref, out_ref, *, devices, rows):
    samples, steps, channels, longitudes = x_ref.shape
    sc = samples * channels
    pieces = [x_ref[s, t] for t in range(steps) for s in range(samples)]
    block = jnp.concatenate(pieces, axis=0)
    coeffs = jnp.dot(block, table_ref[...], preferred_element_type=jnp.float32)
    coeffs = coeffs.astype(jnp.bfloat16)
    for t in range(steps):
        turned = coeffs[t * sc : (t + 1) * sc].T
        for d in range(devices):
            parts = [turned[(4 * d + q) * rows : (4 * d + q + 1) * rows] for q in range(4)]
            out_ref[d, t] = jnp.concatenate(parts, axis=1)


def inverse_kernel(scale_ref, band_ref, table_ref, out_ref):
    devices, steps, rows, lanes = band_ref.shape
    samples, _, channels, longitudes = out_ref.shape
    sc = lanes // 4
    turned = []
    for t in range(steps):
        parts = []
        for d in range(devices):
            block = band_ref[d, t]
            parts += [block[:, q * sc : (q + 1) * sc] for q in range(4)]
        turned.append(jnp.concatenate(parts, axis=0).T)
    block = jnp.concatenate(turned, axis=0)
    values = jnp.dot(block, table_ref[...], preferred_element_type=jnp.float32)
    start = pl.program_id(0) * steps
    for t in range(steps):
        scale = scale_ref[start + t]
        for s in range(samples):
            row = t * sc + s * channels
            out_ref[s, t] = (values[row : row + channels] * scale).astype(jnp.bfloat16)


def middle_kernel(low_ref, legendre_ref, coeffs_ref, gains_ref, out_ref, *, samples):
    legendre = legendre_ref[0]
    packed_rows = legendre.shape[1]
    half = coeffs_ref.shape[2] // 2
    sc = half // 2
    channels = sc // samples
    contract = (((0,), (0,)), ((), ()))
    spectrum = lax.dot_general(legendre, coeffs_ref[0], contract, preferred_element_type=jnp.float32)
    row_ids = lax.broadcasted_iota(jnp.int32, (packed_rows, half), 0)
    inside = row_ids < M - low_ref[pl.program_id(0)]
    own = jnp.where(inside, spectrum[:, :half], spectrum[:, half:])
    other = jnp.concatenate([own[:, sc:], own[:, :sc]], axis=1)
    gains = gains_ref[0]
    gain_re = gains[:, :channels]
    gain_im = gains[:, channels:]
    gain_re = jnp.concatenate([gain_re] * (2 * samples), axis=1)
    gain_im = jnp.concatenate([gain_im] * samples + [-gain_im] * samples, axis=1)
    filtered = gain_re * own + gain_im * other
    zeros = jnp.zeros_like(filtered)
    split = jnp.concatenate([jnp.where(inside, filtered, zeros), jnp.where(inside, zeros, filtered)], axis=1)
    synthesis = jnp.dot(legendre, split.astype(jnp.bfloat16), preferred_element_type=jnp.float32)
    out_ref[0] = synthesis.astype(jnp.bfloat16)


def body(grad_out, legendre, filter_re, filter_im, quad_weight, pair_order, *, devices):
    samples, channels, lat_local, longitudes = grad_out.shape
    pairs_dev, _, packed_rows = legendre.shape
    rows = -(-pairs_dev // 16) * 16
    lanes = 4 * samples * channels
    columns = devices * 4 * rows
    steps = step_of(lat_local, 10)
    whole = lax.all_gather(legendre, "chan", axis=1, tiled=True)
    forward, inverse = basis_tables(pair_order, devices, rows)
    grid_block = pl.BlockSpec((samples, steps, channels, longitudes), lambda i: (0, i, 0, 0))
    band_block = pl.BlockSpec((devices, steps, rows, lanes), lambda i: (0, i, 0, 0))
    params = pltpu.CompilerParams(dimension_semantics=("arbitrary",), vmem_limit_bytes=56 << 20)
    coeffs = pl.pallas_call(
        functools.partial(forward_kernel, devices=devices, rows=rows),
        grid=(lat_local // steps,),
        in_specs=[grid_block, pl.BlockSpec((longitudes, columns), lambda i: (0, 0))],
        out_specs=band_block,
        out_shape=jax.ShapeDtypeStruct((devices, lat_local, rows, lanes), jnp.bfloat16),
        compiler_params=params,
        name="fourier",
    )(jnp.transpose(grad_out, (0, 2, 1, 3)), forward)
    gathered = lax.all_to_all(coeffs, "order", split_axis=0, concat_axis=0, tiled=True)
    latitudes = devices * lat_local
    gathered = gathered.reshape(latitudes, rows, lanes)[:, :pairs_dev]
    gathered = jnp.transpose(gathered, (1, 0, 2))
    start_slot = lax.axis_index("order") * pairs_dev
    low_order = lax.dynamic_slice_in_dim(pair_order, start_slot, pairs_dev)
    gains = pair_gains(low_order, filter_re, filter_im, packed_rows)
    synthesis = pl.pallas_call(
        functools.partial(middle_kernel, samples=samples),
        grid=(pairs_dev,),
        in_specs=[
            pl.BlockSpec(memory_space=pltpu.SMEM),
            pl.BlockSpec((1, latitudes, packed_rows), lambda i: (i, 0, 0)),
            pl.BlockSpec((1, latitudes, lanes), lambda i: (i, 0, 0)),
            pl.BlockSpec((1, packed_rows, 2 * channels), lambda i: (i, 0, 0)),
        ],
        out_specs=pl.BlockSpec((1, latitudes, lanes), lambda i: (i, 0, 0)),
        out_shape=jax.ShapeDtypeStruct((pairs_dev, latitudes, lanes), jnp.bfloat16),
        compiler_params=params,
        name="legendre",
    )(low_order, whole, gathered, gains)
    synthesis = jnp.transpose(synthesis, (1, 0, 2))
    synthesis = jnp.pad(synthesis, ((0, 0), (0, rows - pairs_dev), (0, 0)))
    synthesis = synthesis.reshape(devices, lat_local, rows, lanes)
    band = lax.all_to_all(synthesis, "order", split_axis=0, concat_axis=0, tiled=True)
    scale = quad_weight * (2.0 * math.pi / NLON)
    values = pl.pallas_call(
        inverse_kernel,
        grid=(lat_local // steps,),
        in_specs=[
            pl.BlockSpec(memory_space=pltpu.SMEM),
            band_block,
            pl.BlockSpec((columns, longitudes), lambda i: (0, 0)),
        ],
        out_specs=grid_block,
        out_shape=jax.ShapeDtypeStruct((samples, lat_local, channels, longitudes), jnp.bfloat16),
        compiler_params=params,
        name="fourier_back",
    )(scale, band, inverse)
    return jnp.transpose(values, (0, 2, 1, 3))


def solution(mesh):
    in_specs = (
        P(None, "chan", "order", None),
        P("order", "chan", None),
        P("chan", None),
        P("chan", None),
        P("order"),
        P(),
    )
    out_specs = P(None, "chan", "order", None)
    local = functools.partial(body, devices=mesh.shape["order"])
    return jax.shard_map(local, mesh=mesh, in_specs=in_specs, out_specs=out_specs, check_vma=False)
```

time: 457 us -> 374 us (0.82); the launches traced: 448 us -> 372 us
  matrix products: 143 us -> 0 us
  Pallas kernels: 0 us -> 92.2 us
  local copies, waits for them, and re-layouts: 90 us -> 44.1 us
  waiting for transfers between devices: 147 us -> 160 us
  other arithmetic: 19 us -> 27.5 us
    dot_general x4 -> x0, matrix products: 143 us -> none  [the longest x1 53.8 us: body(): jnp.einsum('sctl,lpq->ptqsc', grad_out, forward, preferred_element_type=j...]
    pallas_call x0 -> x3, Pallas kernels: none -> 92.2 us  [the longest x1 33.6 us: body(): pl.pallas_call(functools.partial(forward_kernel, devices=devices, rows=ro...]
    convert_element_type x2 -> x0, local copies, waits for them, and re-layouts: 43.7 us -> none  [the longest x1 35.6 us: body(): return (values * scale[None, None, :, None]).astype(jnp.bfloat16)]
    all_to_all x3 -> x0, local copies, waits for them, and re-layouts: 28.9 us -> none  [the longest x2 16.2 us: body(): lax.all_to_all(coeffs, 'order', split_axis=0, concat_axis=1, tiled=True)]
    unnamed x9 -> x16, local copies, waits for them, and re-layouts: 3.79 us -> 20.1 us
    convert_element_type x0 -> x2, other arithmetic: none -> 15.3 us  [the longest x1 8.08 us: basis_tables(): return (forward, inverse.astype(jnp.bfloat16))]
    all_gather x0 -> x1, local copies, waits for them, and re-layouts: none -> 14.7 us  [body(): whole = lax.all_gather(legendre, 'chan', axis=1, tiled=True)]
    reshape x1 -> x0, local copies, waits for them, and re-layouts: 12.5 us -> none  [body(): coeffs.astype(jnp.bfloat16)]
  transfers between devices with their start and end apart: 3 -> 3, of which waited for: 2 -> 3; matrix products, arithmetic and copies ran while one was open for 18% -> 10% of each run, Pallas kernels for 0% -> 9%
where the time goes in v1:
time: 374 us; the launch traced here: 372 us
  waiting for transfers between devices  160 us (43%)
  Pallas kernels  92.2 us (25%)
  local copies, waits for them, and re-layouts  44.1 us (12%)
  between operations  36 us (10%)
  other arithmetic  27.5 us (7%)
  starting transfers between devices  11.9 us (3%)
    all_to_all x1, waiting for transfers between devices, body(): lax.all_to_all(synthesis, 'order', split_axis=0, concat_axis=0, tiled=True)  89.4 us
    all_to_all x1, waiting for transfers between devices, body(): lax.all_to_all(coeffs, 'order', split_axis=0, concat_axis=0, tiled=True)  63.8 us
    pallas_call x1, Pallas kernels, body(): pl.pallas_call(functools.partial(forward_kernel, devices=devices, rows=ro...  33.6 us
    pallas_call x1, Pallas kernels, body(): pl.pallas_call(functools.partial(middle_kernel, samples=samples), grid=(p...  29.4 us
    pallas_call x1, Pallas kernels, body(): pl.pallas_call(inverse_kernel, grid=(lat_local // steps,), in_specs=[pl.B...  29.2 us
    unnamed x16, local copies, waits for them, and re-layouts  20.1 us
    all_gather x1, local copies, waits for them, and re-layouts, body(): whole = lax.all_gather(legendre, 'chan', axis=1, tiled=True)  14.7 us
    unnamed x11, other arithmetic  10.3 us
  transfers between devices with their start and end apart: 3, of which 3 were waited for; matrix products, arithmetic and copies ran while one was open for 10% of the time, Pallas kernels for 9%

profile of v1, /device:TPU:0, one launch (start us, length us, event | category | flops | bytes accessed | tf_op | source)
XLA Modules:
  0.0 372.1 jit_solution(7717177332331776054)
XLA Ops:
  6.5 3.8 %copy.16 = bf16[12,90,768]{2,0,1:T(8,128)(2,1)} copy(bf16[12,90,768]{2,1,0:T(8,128)(2,1)} %param.7) | data formatting | bytes 3317760 | tf_op args[1]
  10.8 7.2 %multiply_convert_fusion.table_ref = bf16[1440,256]{1,0:T(8,128)(2,1)} fusion(f32[256]{0:T(256)S(1)} %compare_select_fusion, s32[256]{0:T(256)S(1)} %mul.54, pred[256]{0:T(512)(128)(4,1)S(1)} %eq.28, pred[256]{0:T(512)(128)(4,1)S(1)} %broadcast_in_dim.137), kind=kLoop, calls=%fused_computation.24 | loop fusion | flops 5160960 | bytes 739840 | tf_op jit(solution)/shard_map/convert_element_type | solution.py:36
  18.1 33.6 %fourier.1 = bf16[4,180,16,384]{3,2,1,0:T(8,128)(2,1)} custom-call(bf16[3,180,32,1440]{3,2,1,0:T(8,128)(2,1)} %bitcast.73, bf16[1440,256]{1,0:T(8,128)(2,1)} %multiply_convert_fusion.table_ref), custom_call_target="tpu_custom_call" | custom-call | tf_op jit(solution)/shard_map/fourier/pallas_call | solution.py:126
  51.7 6.1 %all-to-all-start = ((bf16[4,180,16,384]{3,2,1,0:T(8,128)(2,1)}), bf16[4,180,16,384]{3,2,1,0:T(8,128)(2,1)}, u32[]{:S(2)}, u32[]{:S(2)}) async-start(bf16[4,180,16,384]{3,2,1,0:T(8,128)(2,1)} %fourier.1), calls=%async_computation | async-start | bytes 17694720 | tf_op jit(solution)/shard_map/all_to_all | solution.py:135
  81.8 0.9 fusion.12
  82.7 0.9 fusion.15
  84.6 1.0 fusion.21
  85.5 0.9 fusion.24
  88.3 0.9 fusion.33
  89.3 0.9 fusion.36
  90.2 0.9 fusion.39
  91.1 0.9 fusion.42
  92.1 0.9 fusion.45.gains_ref
  93.0 63.8 %all-to-all-done = bf16[4,180,16,384]{3,2,1,0:T(8,128)(2,1)} async-done(((bf16[4,180,16,384]{3,2,1,0:T(8,128)(2,1)}), bf16[4,180,16,384]{3,2,1,0:T(8,128)(2,1)}, u32[]{:S(2)}, u32[]{:S(2)}) %all-to-all-start) | async-done | bytes 8847392 | tf_op jit(solution)/shard_map/all_to_all | solution.py:135
  156.8 7.8 %copy.27 = bf16[720,12,384]{2,0,1:T(8,128)(2,1)} copy(bf16[720,12,384]{2,1,0:T(8,128)(2,1)} %bitcast.72) | data formatting | bytes 13271040
  164.6 7.2 %all-gather.2.cloned.1.call-done = bf16[12,720,768]{2,0,1:T(8,128)(2,1)} async-done(((bf16[12,90,768]{2,0,1:T(8,128)(2,1)}), bf16[12,720,768]{2,0,1:T(8,128)(2,1)}) %all-gather.2.cloned.1.call-update) | async-done | bytes 13271056 | tf_op jit(solution)/shard_map/all_gather | solution.py:121
  171.8 14.7 %copy.21.legendre_ref = bf16[12,720,768]{2,1,0:T(8,128)(2,1)} copy(bf16[12,720,768]{2,0,1:T(8,128)(2,1)} %all-gather.2.cloned.1.call-done) | data formatting | bytes 26542080 | tf_op jit(solution)/shard_map/all_gather | solution.py:121
  186.6 29.4 %legendre.1 = bf16[12,720,384]{2,1,0:T(8,128)(2,1)} custom-call(s32[12]{0:T(128)} %copy-done, bf16[12,720,768]{2,1,0:T(8,128)(2,1)} %copy.21.legendre_ref, bf16[12,720,384]{2,1,0:T(8,128)(2,1)} %bitcast.75, f32[12,768,64]{2,1,0:T(8,128)} %fusion.45.gains_ref), custom_call_target="tpu_custom_call" | custom-call | tf_op jit(solution)/shard_map/legendre/pallas_call | solution.py:142
  215.9 8.1 %copy.25 = bf16[720,12,384]{2,1,0:T(8,128)(2,1)} copy(bf16[720,12,384]{2,0,1:T(8,128)(2,1)} %bitcast.76) | data formatting | bytes 13271040
  224.1 8.1 %pad.10.clone = bf16[720,16,384]{2,1,0:T(8,128)(2,1)} pad(bf16[720,12,384]{2,1,0:T(8,128)(2,1)} %copy.25, bf16[]{:T(256)} %constant.57.clone.1), padding=0_0x0_4x0_0 | pad | bytes 15482882 | tf_op jit(solution)/shard_map/jit(_pad)/pad | solution.py:157
  232.2 5.9 %all-to-all-start.1 = ((bf16[4,180,16,384]{3,2,1,0:T(8,128)(2,1)}), bf16[4,180,16,384]{3,2,1,0:T(8,128)(2,1)}, u32[]{:S(2)}, u32[]{:S(2)}) async-start(bf16[4,180,16,384]{3,2,1,0:T(8,128)(2,1)} %bitcast.74), calls=%async_computation.1 | async-start | bytes 17694720 | tf_op jit(solution)/shard_map/all_to_all | solution.py:159
  238.6 8.1 %select_convert_fusion.table_ref = bf16[256,1440]{1,0:T(8,128)(2,1)} fusion(s32[256]{0:T(256)S(1)} %mul.54, pred[256]{0:T(512)(128)(4,1)S(1)} %eq.28, pred[256]{0:T(512)(128)(4,1)S(1)} %broadcast_in_dim.137), kind=kLoop, calls=%fused_computation.17 | loop fusion | flops 4792320 | bytes 738816 | tf_op jit(solution)/shard_map/convert_element_type | solution.py:37
  246.7 89.4 %all-to-all-done.1.band_ref = bf16[4,180,16,384]{3,2,1,0:T(8,128)(2,1)} async-done(((bf16[4,180,16,384]{3,2,1,0:T(8,128)(2,1)}), bf16[4,180,16,384]{3,2,1,0:T(8,128)(2,1)}, u32[]{:S(2)}, u32[]{:S(2)}) %all-to-all-start.1) | async-done | bytes 8847392 | tf_op jit(solution)/shard_map/all_to_all | solution.py:159
  336.1 29.2 %fourier_back.1 = bf16[3,180,32,1440]{3,2,1,0:T(8,128)(2,1)} custom-call(f32[180]{0:T(256)} %broadcast_multiply_fusion.scale_ref, bf16[4,180,16,384]{3,2,1,0:T(8,128)(2,1)} %all-to-all-done.1.band_ref, bf16[256,1440]{1,0:T(8,128)(2,1)} %select_convert_fusion.table_ref), custom_call_target="tpu_custom_call" | custom-call | tf_op jit(solution)/shard_map/fourier_back/pallas_call | solution.py:161
  (39 shorter events, 5.3 us)
Async XLA Ops:
  6.5 4.1 %copy-start.3 = (s32[48]{0:T(128)S(1)}, s32[48]{0:T(128)}, u32[]{:S(2)}) copy-start(s32[48]{0:T(128)} %param.11) | copy-start | bytes 580
  6.5 165.3 %all-gather.2.cloned.1.call-start = ((), (), s32[]{:S(2)}) async-start(), calls=%async_computation.2 | async-start | bytes 19906560 | tf_op jit(solution)/shard_map/all_gather | solution.py:121
  51.7 21.9 %copy-start.1 = (f32[32,720]{1,0:T(8,128)S(1)}, f32[32,720]{1,0:T(8,128)}, u32[]{:S(2)}) copy-start(f32[32,720]{1,0:T(8,128)} %param.8) | copy-start | bytes 276484
  51.7 22.0 %copy-start.2 = (f32[32,720]{1,0:T(8,128)S(1)}, f32[32,720]{1,0:T(8,128)}, u32[]{:S(2)}) copy-start(f32[32,720]{1,0:T(8,128)} %param.9) | copy-start | bytes 276484
  51.7 105.1 %all-to-all-start = ((bf16[4,180,16,384]{3,2,1,0:T(8,128)(2,1)}), bf16[4,180,16,384]{3,2,1,0:T(8,128)(2,1)}, u32[]{:S(2)}, u32[]{:S(2)}) async-start(bf16[4,180,16,384]{3,2,1,0:T(8,128)(2,1)} %fourier.1), calls=%async_computation | async-start | bytes 17694720 | tf_op jit(solution)/shard_map/all_to_all | solution.py:135
  57.9 33.3 %copy-start = (s32[12]{0:T(128)}, s32[12]{0:T(128)S(1)}, u32[]{:S(2)}) copy-start(s32[12]{0:T(128)S(1)} %get-tuple-element.18.low_ref) | copy-start | bytes 148
  232.2 5.9 %copy-start.4 = (f32[180]{0:T(256)S(1)}, f32[180]{0:T(256)}, u32[]{:S(2)}) copy-start(f32[180]{0:T(256)} %param.10) | copy-start | bytes 2164
  232.2 103.9 %all-to-all-start.1 = ((bf16[4,180,16,384]{3,2,1,0:T(8,128)(2,1)}), bf16[4,180,16,384]{3,2,1,0:T(8,128)(2,1)}, u32[]{:S(2)}, u32[]{:S(2)}) async-start(bf16[4,180,16,384]{3,2,1,0:T(8,128)(2,1)} %bitcast.74), calls=%async_computation.1 | async-start | bytes 17694720 | tf_op jit(solution)/shard_map/all_to_all | solution.py:159
Sparse Core Ops, SparseCore 0:
  10.5 161.3 all-gather.1
